TPU v7x, 128 devices: a whole 4x4x4 slice. The times are simulated.
128 devices in a mesh: expert: 64 (over z, y, x_hi, core), dp: 2 (over x_lo).
Axes of the slice: x: 4 (x_hi: 2, x_lo: 2; x = x_hi * 2 + x_lo), y: 4, z: 4, core: 2. Of those that a mesh axis runs over, the one named last changes fastest.
Arguments:
- tokens: bfloat16 [8192, 4096], P(('expert', 'dp')), may hold values from -6 to 6
- expert_ids: int32 [8192, 8], P(('expert', 'dp')), may hold values from 0 to 127, all different within a row; in each aligned block of 64 rows (0 to 63, 64 to 127, ...) at most 8 rows name the same one
- gate_up: bfloat16 [128, 4096, 1536], P('expert', None, 'dp'), may hold values from -0.09375 to 0.09375
Outputs:
- factors: float32 [128, 768, 768], P('expert', 'dp')
Inputs may be any that keep to these rules, and one draw needn't show every extreme that they name: `expert_ids`: each token names 8 distinct experts. Within each device's aligned block of 64 tokens no expert is named more than 8 times, a bound that some block reaches.
All inputs are finite; a program needn't handle non-finite values.
Results may differ from a plain program's by a relative error of at most 0.004.
Values may be sent and summed in bfloat16 or wider, within the bound.
A program may use at most 192 MiB of HBM per device.

v0:
```python
import jax
import jax.numpy as jnp
from jax import lax
from jax.sharding import PartitionSpec as P

damping = 0.25


def project(rows, weight):
    return jnp.einsum("esd,edc->esc", rows, weight, preferred_element_type=jnp.float32)


def swiglu(both, width):
    return (jax.nn.silu(both[:, :, :width]) * both[:, :, width:]).astype(jnp.bfloat16)


def second_moment(hidden, scale, extra):
    gram = jnp.einsum("esf,esg->efg", hidden, hidden, preferred_element_type=jnp.float32)
    identity = jnp.eye(hidden.shape[2], dtype=jnp.float32)
    return gram * scale + extra * identity[None]


def upper_factor(moment):
    return jnp.swapaxes(jnp.linalg.cholesky(moment), 1, 2)


def on_device(tokens, expert_ids, gate_up):
    expert_axis = lax.axis_size("expert")
    replicas = lax.axis_size("dp")
    local_count = gate_up.shape[0]
    expert_count = local_count * expert_axis
    token_count, top_count = expert_ids.shape
    width_full = gate_up.shape[2] * replicas // 2
    width_part = width_full // replicas
    capacity = 2 * token_count * top_count // expert_count
    rows_mean = token_count * expert_axis * replicas * top_count // expert_count
    scale = 1.0 / rows_mean
    extra = damping * damping / replicas
    flat_ids = expert_ids.reshape(-1)
    onehot = (flat_ids[:, None] == jnp.arange(expert_count, dtype=jnp.int32)[None, :]).astype(
        jnp.int32
    )
    ranking = jnp.sum((jnp.cumsum(onehot, axis=0) - 1) * onehot, axis=1)
    target = flat_ids * capacity + ranking
    placing = jnp.arange(expert_count * capacity, dtype=jnp.int32)[:, None] == target[None, :]
    placing = jnp.any(
        placing.reshape(expert_count * capacity, token_count, top_count), axis=2
    ).astype(jnp.bfloat16)
    outgoing = jnp.dot(placing, tokens, preferred_element_type=jnp.float32).astype(jnp.bfloat16)
    outgoing = outgoing.reshape(expert_count, capacity, tokens.shape[1])
    arrived = lax.all_to_all(outgoing, "expert", split_axis=0, concat_axis=1, tiled=True)
    both = project(arrived, lax.all_gather(gate_up, "dp", axis=2, tiled=True))
    hidden = swiglu(both, width_full)
    local_moment = second_moment(hidden, scale, extra)
    total_moment = lax.psum(local_moment, "dp")
    factor = upper_factor(total_moment)
    position = lax.axis_index("dp")
    return lax.dynamic_slice_in_dim(factor, position * width_part, width_part, 1)


def solution(mesh):
    return jax.shard_map(
        on_device,
        mesh=mesh,
        in_specs=(P(("expert", "dp"), None), P(("expert", "dp"), None), P("expert", None, "dp")),
        out_specs=P("expert", "dp", None),
        check_vma=False,
    )
```

profile of v0, /device:TPU:1, one launch (start us, length us, event | category | flops | bytes accessed | tf_op | source)
XLA Modules:
  0.0 836.7 jit_solution(10531696009400579675)
XLA Ops:
  6.5 0.7 all-gather.2.cloned.1.call-update
  7.7 0.2 fusion.23
  8.0 0.2 fusion.22
  8.5 0.7 fusion.8
  9.2 5.6 convert_bitcast_fusion
  14.8 12.7 %all-to-all-start = ((bf16[128,8,4096]{2,1,0:T(8,128)(2,1)}), bf16[128,8,4096]{2,1,0:T(8,128)(2,1)}, u32[]{:S(2)}, u32[]{:S(2)}) async-start(bf16[128,8,4096]{2,1,0:T(8,128)(2,1)} %convert_bitcast_fusion), calls=%async_computation | async-start | bytes 16777216 | tf_op jit(solution)/shard_map/all_to_all | solution.py:51
  27.5 0.2 all-reduce.3.cloned.1.call-start
  27.7 0.2 fusion.7
  27.9 176.4 %all-to-all-done = bf16[128,8,4096]{2,1,0:T(8,128)(2,1)} async-done(((bf16[128,8,4096]{2,1,0:T(8,128)(2,1)}), bf16[128,8,4096]{2,1,0:T(8,128)(2,1)}, u32[]{:S(2)}, u32[]{:S(2)}) %all-to-all-start) | async-done | bytes 8388640 | tf_op jit(solution)/shard_map/all_to_all | solution.py:51
  204.2 184.2 %all-gather.2.cloned.1.call-done = bf16[2,4096,1536]{2,1,0:T(8,128)(2,1)} async-done(((bf16[2,4096,768]{2,1,0:T(8,128)(2,1)}), bf16[2,4096,1536]{2,1,0:T(8,128)(2,1)}) %all-gather.2.cloned.1.call-update) | async-done | bytes 25165840 | tf_op jit(solution)/shard_map/all_gather | solution.py:52
  388.4 20.7 %fusion = f32[2,512,1536]{2,1,0:T(8,128)} fusion(bf16[2,4096,1536]{2,1,0:T(8,128)(2,1)} %all-gather.2.cloned.1.call-done, bf16[64,2,8,4096]{3,2,1,0:T(8,128)(2,1)} %bitcast.4), kind=kOutput, calls=%fused_computation | convolution fusion | flops 12884901888 | bytes 39845888 | tf_op jit(solution)/shard_map/esd,edc->esc/dot_general | solution.py:10
  409.2 9.1 %multiply_add_fusion = f32[2,768,768]{1,2,0:T(8,128)} fusion(f32[768,768]{0,1:T(8,128)S(1)} %fusion.7, f32[2,512,1536]{2,1,0:T(8,128)} %fusion), kind=kOutput, calls=%fused_computation.6 | convolution fusion | flops 1215037440 | bytes 13369344 | tf_op jit(solution)/shard_map/esf,esg->efg/dot_general | solution.py:18
  418.4 0.2 iota_compare_fusion.1
  418.6 128.3 %all-reduce.3.cloned.1.call-done = f32[2,768,768]{1,2,0:T(8,128)} async-done(((f32[2,768,768]{1,2,0:T(8,128)}), f32[2,768,768]{1,2,0:T(8,128)}) %all-reduce.3.cloned.1.call-update) | async-done | bytes 4718608 | tf_op jit(solution)/shard_map/psum | solution.py:55
  546.9 6.2 copy.71
  553.1 4.4 fusion.3
  557.4 2.1 copy-done.2
  559.6 23.5 %custom-call.49 = f32[2,128,128]{2,1,0:T(8,128)S(1)} custom-call(f32[2,128,128]{2,1,0:T(8,128)S(1)} %cholesky.426), custom_call_target="Cholesky" | custom-call | tf_op jit(solution)/shard_map/jit(cholesky)/cholesky | solution.py:24
  583.1 19.9 %custom-call.50 = f32[2,1,128,128]{2,3,1,0:T(8,128)S(1)} custom-call(f32[2,1,128,128]{3,2,1,0:T(8,128)S(1)} %select_bitcast_fusion.4), custom_call_target="InvertDiagBlocksLowerTriangular" | custom-call | tf_op jit(solution)/shard_map/jit(cholesky)/cholesky | solution.py:24
  602.9 2.5 cholesky.197
  605.4 2.8 constant_dynamic-update-slice_fusion.5
  608.2 1.8 convolution_subtract_fusion
  610.0 23.5 %custom-call.51 = f32[2,128,128]{2,1,0:T(8,128)S(1)} custom-call(f32[2,128,128]{2,1,0:T(8,128)S(1)} %cholesky.430), custom_call_target="Cholesky" | custom-call | tf_op jit(solution)/shard_map/jit(cholesky)/cholesky | solution.py:24
  633.5 0.7 select_bitcast_fusion.3
  634.2 19.7 %custom-call.52 = f32[2,1,128,128]{2,3,1,0:T(8,128)S(1)} custom-call(f32[2,1,128,128]{3,2,1,0:T(8,128)S(1)} %get-tuple-element.18), custom_call_target="InvertDiagBlocksLowerTriangular" | custom-call | tf_op jit(solution)/shard_map/jit(cholesky)/cholesky | solution.py:24
  653.9 1.4 convolution_dynamic-update-slice_fusion
  655.3 2.5 convolution_subtract_fusion.1
  657.9 23.9 %custom-call.53 = f32[2,128,128]{2,1,0:T(8,128)S(1)} custom-call(f32[2,128,128]{2,1,0:T(8,128)S(1)} %cholesky.435), custom_call_target="Cholesky" | custom-call | tf_op jit(solution)/shard_map/jit(cholesky)/cholesky | solution.py:24
  681.7 0.7 select_bitcast_fusion.2
  682.4 19.7 %custom-call.54 = f32[2,1,128,128]{2,3,1,0:T(8,128)S(1)} custom-call(f32[2,1,128,128]{3,2,1,0:T(8,128)S(1)} %get-tuple-element.16), custom_call_target="InvertDiagBlocksLowerTriangular" | custom-call | tf_op jit(solution)/shard_map/jit(cholesky)/cholesky | solution.py:24
  702.1 1.3 convolution_dynamic-update-slice_fusion.1
  703.4 2.7 convolution_subtract_fusion.2
  706.1 23.5 %custom-call.55 = f32[2,128,128]{2,1,0:T(8,128)S(1)} custom-call(f32[2,128,128]{2,1,0:T(8,128)S(1)} %cholesky.440), custom_call_target="Cholesky" | custom-call | tf_op jit(solution)/shard_map/jit(cholesky)/cholesky | solution.py:24
  729.6 0.7 select_bitcast_fusion.1
  730.3 19.8 %custom-call.56 = f32[2,1,128,128]{2,3,1,0:T(8,128)S(1)} custom-call(f32[2,1,128,128]{3,2,1,0:T(8,128)S(1)} %get-tuple-element.14), custom_call_target="InvertDiagBlocksLowerTriangular" | custom-call | tf_op jit(solution)/shard_map/jit(cholesky)/cholesky | solution.py:24
  750.1 1.1 convolution_dynamic-update-slice_fusion.2
  751.2 2.5 convolution_subtract_fusion.3
  753.8 23.5 %custom-call.57 = f32[2,128,128]{2,1,0:T(8,128)S(1)} custom-call(f32[2,128,128]{2,1,0:T(8,128)S(1)} %cholesky.445), custom_call_target="Cholesky" | custom-call | tf_op jit(solution)/shard_map/jit(cholesky)/cholesky | solution.py:24
  777.2 0.7 select_bitcast_fusion
  777.9 19.7 %custom-call.58 = f32[2,1,128,128]{2,3,1,0:T(8,128)S(1)} custom-call(f32[2,1,128,128]{3,2,1,0:T(8,128)S(1)} %get-tuple-element.12), custom_call_target="InvertDiagBlocksLowerTriangular" | custom-call | tf_op jit(solution)/shard_map/jit(cholesky)/cholesky | solution.py:24
  797.6 0.9 convolution_dynamic-update-slice_fusion.3
  798.5 2.2 convolution_subtract_fusion.4
  800.7 23.7 %custom-call.59 = f32[2,128,128]{2,1,0:T(8,128)S(1)} custom-call(f32[2,128,128]{2,1,0:T(8,128)S(1)} %convolution_subtract_fusion.4), custom_call_target="Cholesky" | custom-call | tf_op jit(solution)/shard_map/jit(cholesky)/cholesky | solution.py:24
  824.4 0.7 select_reduce_fusion.4
  825.3 0.2 compare_reduce_fusion.2
  825.4 0.2 compare_reduce_fusion
  825.6 2.1 fusion.6
  827.7 2.0 copy.82
  (33 shorter events, 1.1 us)
Async XLA Ops:
  6.5 2.7 copy-start
  6.5 0.7 copy-start.3
  6.5 381.9 %all-gather.2.cloned.1.call-start = ((), (), s32[]{:S(2)}) async-start(), calls=%async_computation.1 | async-start | bytes 37748736 | tf_op jit(solution)/shard_map/all_gather | solution.py:52
  14.8 189.4 %all-to-all-start = ((bf16[128,8,4096]{2,1,0:T(8,128)(2,1)}), bf16[128,8,4096]{2,1,0:T(8,128)(2,1)}, u32[]{:S(2)}, u32[]{:S(2)}) async-start(bf16[128,8,4096]{2,1,0:T(8,128)(2,1)} %convert_bitcast_fusion), calls=%async_computation | async-start | bytes 16777216 | tf_op jit(solution)/shard_map/all_to_all | solution.py:51
  27.5 519.4 %all-reduce.3.cloned.1.call-start = ((), (), s32[]{:S(2)}) async-start(), calls=%async_computation.2 | async-start | bytes 9437184 | tf_op jit(solution)/shard_map/psum | solution.py:55
  557.4 2.1 copy-start.2
  825.6 4.1 copy-start.1
Sparse Core Ops, SparseCore 0:
  9.0 379.3 all-gather.1
  418.4 128.4 all-reduce.2
where the time goes:
time: 841 us; the launch traced here: 837 us
  waiting for transfers between devices  490 us (58%)
  other arithmetic  252 us (30%)
  matrix products  54.7 us (7%)
  between operations  13.9 us (2%)
  local copies, waits for them, and re-layouts  13.5 us (2%)
  starting transfers between devices  12.9 us (2%)
    another operation x23, other arithmetic, upper_factor(): return jnp.swapaxes(jnp.linalg.cholesky(moment), 1, 2)  244 us
    all_gather x1, waiting for transfers between devices, on_device(): both = project(arrived, lax.all_gather(gate_up, 'dp', axis=2, tiled=True))  184 us
    all_to_all x1, waiting for transfers between devices, on_device(): lax.all_to_all(outgoing, 'expert', split_axis=0, concat_axis=1, tiled=True)  176 us
    psum x1, waiting for transfers between devices, on_device(): total_moment = lax.psum(local_moment, 'dp')  128 us
    dot_general x1, matrix products, project(): jnp.einsum('esd,edc->esc', rows, weight, preferred_element_type=jnp.float32)  20.7 us
    another operation x10, matrix products, upper_factor(): return jnp.swapaxes(jnp.linalg.cholesky(moment), 1, 2)  19.3 us
  transfers between devices with their start and end apart: 3, of which 3 were waited for; matrix products, arithmetic and copies ran while one was open for 1% of the time, Pallas kernels for 0%

commit v1 on v0

--- a/solution.py
+++ b/solution.py
@@ -1,9 +1,20 @@
+import functools
 import jax
 import jax.numpy as jnp
 from jax import lax
 from jax.sharding import PartitionSpec as P
+from jax.lax import all_to_all, axis_size
 
 damping = 0.25
+
+
+def sample_open(local_block, mesh_ax):
+    out_arr = jnp.stack([local_block for _ in range(axis_size(mesh_ax))])
+    heard = jnp.concatenate(all_to_all(out_arr, mesh_ax, 0, 0), 2)
+    return heard
+
+
+_build_edge = functools.partial(sample_open, mesh_ax="dp")
 
 
 def project(rows, weight):
@@ -49,7 +60,7 @@
     outgoing = jnp.dot(placing, tokens, preferred_element_type=jnp.float32).astype(jnp.bfloat16)
     outgoing = outgoing.reshape(expert_count, capacity, tokens.shape[1])
     arrived = lax.all_to_all(outgoing, "expert", split_axis=0, concat_axis=1, tiled=True)
-    both = project(arrived, lax.all_gather(gate_up, "dp", axis=2, tiled=True))
+    both = project(arrived, _build_edge(gate_up))
     hidden = swiglu(both, width_full)
     local_moment = second_moment(hidden, scale, extra)
     total_moment = lax.psum(local_moment, "dp")

time: 841 us -> 889 us (1.057)
  other arithmetic: 252 us -> 273 us
  local copies, waits for them, and re-layouts: 13.5 us -> 34.5 us
  starting transfers between devices: 12.9 us -> 25.5 us
    all_to_all x0 -> x1, waiting for transfers between devices: none -> 264 us  [sample_open(): heard = jnp.concatenate(all_to_all(out_arr, mesh_ax, 0, 0), 2)]
    all_gather x1 -> x0, waiting for transfers between devices: 184 us -> none  [on_device(): both = project(arrived, lax.all_gather(gate_up, 'dp', axis=2, tiled=True))]
    all_to_all x1, waiting for transfers between devices: 176 us -> 78.5 us  [on_device(): lax.all_to_all(outgoing, 'expert', split_axis=0, concat_axis=1, tiled=True)]
    reshape x0 -> x1, local copies, waits for them, and re-layouts: none -> 21 us  [sample_open(): heard = jnp.concatenate(all_to_all(out_arr, mesh_ax, 0, 0), 2)]
    another operation x2 -> x3, other arithmetic: 0.24 us -> 21 us  [the longest x1 20.8 us: sample_open(): out_arr = jnp.stack([local_block for _ in range(axis_size(mesh_ax))])]
    all_to_all x0 -> x1, starting transfers between devices: none -> 11.9 us  [sample_open(): heard = jnp.concatenate(all_to_all(out_arr, mesh_ax, 0, 0), 2)]
    psum x1, waiting for transfers between devices: 128 us -> 140 us  [on_device(): total_moment = lax.psum(local_moment, 'dp')]
  transfers between devices with their start and end apart: 3 -> 3, of which waited for: 3 -> 3; matrix products, arithmetic and copies ran while one was open for 1% -> 3% of each run, Pallas kernels for 0% -> 0%
where the time goes in v1:
time: 889 us; the launch traced here: 884 us
  waiting for transfers between devices  483 us (54%)
  other arithmetic  273 us (31%)
  matrix products  54.7 us (6%)
  local copies, waits for them, and re-layouts  34.5 us (4%)
  starting transfers between devices  25.5 us (3%)
  between operations  13.9 us (2%)
    all_to_all x1, waiting for transfers between devices, sample_open(): heard = jnp.concatenate(all_to_all(out_arr, mesh_ax, 0, 0), 2)  264 us
    another operation x23, other arithmetic, upper_factor(): return jnp.swapaxes(jnp.linalg.cholesky(moment), 1, 2)  244 us
    psum x1, waiting for transfers between devices, on_device(): total_moment = lax.psum(local_moment, 'dp')  140 us
    all_to_all x1, waiting for transfers between devices, on_device(): lax.all_to_all(outgoing, 'expert', split_axis=0, concat_axis=1, tiled=True)  78.5 us
    reshape x1, local copies, waits for them, and re-layouts, sample_open(): heard = jnp.concatenate(all_to_all(out_arr, mesh_ax, 0, 0), 2)  21 us
    another operation x1, other arithmetic, sample_open(): out_arr = jnp.stack([local_block for _ in range(axis_size(mesh_ax))])  20.8 us
    dot_general x1, matrix products, project(): jnp.einsum('esd,edc->esc', rows, weight, preferred_element_type=jnp.float32)  20.6 us
    another operation x10, matrix products, upper_factor(): return jnp.swapaxes(jnp.linalg.cholesky(moment), 1, 2)  19.3 us
  transfers between devices with their start and end apart: 3, of which 3 were waited for; matrix products, arithmetic and copies ran while one was open for 3% of the time, Pallas kernels for 0%

profile of v1, /device:TPU:1, one launch (start us, length us, event | category | flops | bytes accessed | tf_op | source)
XLA Modules:
  0.0 884.3 jit_solution(2649171574555066523)
XLA Ops:
  6.5 20.8 %pad_maximum_fusion = bf16[2,2,4096,768]{3,2,1,0:T(8,128)(2,1)} fusion(bf16[1,2,4096,768]{3,2,1,0:T(8,128)(2,1)} %bitcast.68), kind=kLoop, calls=%fused_computation | loop fusion | flops 12582912 | bytes 37748736 | tf_op jit(solution)/shard_map/stack | solution.py:12
  27.3 11.9 %all-to-all-start.1 = ((bf16[2,2,4096,768]{3,2,1,0:T(8,128)(2,1)}), bf16[2,2,4096,768]{3,2,1,0:T(8,128)(2,1)}, u32[]{:S(2)}, u32[]{:S(2)}) async-start(bf16[2,2,4096,768]{3,2,1,0:T(8,128)(2,1)} %pad_maximum_fusion), calls=%async_computation.1 | async-start | bytes 50331648 | tf_op jit(solution)/shard_map/all_to_all | solution.py:13
  39.6 0.2 fusion.23
  40.0 0.2 fusion.22
  40.5 0.7 fusion.8
  41.2 5.6 convert_bitcast_fusion
  46.8 264.1 %all-to-all-done.1 = bf16[2,2,4096,768]{3,2,1,0:T(8,128)(2,1)} async-done(((bf16[2,2,4096,768]{3,2,1,0:T(8,128)(2,1)}), bf16[2,2,4096,768]{3,2,1,0:T(8,128)(2,1)}, u32[]{:S(2)}, u32[]{:S(2)}) %all-to-all-start.1) | async-done | bytes 25165856 | tf_op jit(solution)/shard_map/all_to_all | solution.py:13
  310.9 13.3 %all-to-all-start = ((bf16[128,8,4096]{2,1,0:T(8,128)(2,1)}), bf16[128,8,4096]{2,1,0:T(8,128)(2,1)}, u32[]{:S(2)}, u32[]{:S(2)}) async-start(bf16[128,8,4096]{2,1,0:T(8,128)(2,1)} %convert_bitcast_fusion), calls=%async_computation | async-start | bytes 16777216 | tf_op jit(solution)/shard_map/all_to_all | solution.py:62
  324.3 0.2 all-reduce.3.cloned.1.call-start
  324.5 0.2 fusion.7
  324.7 21.0 %copy.94 = bf16[2,2,512,8,768]{4,3,0,2,1:T(8,128)(2,1)} copy(bf16[2,2,512,8,768]{4,3,2,1,0:T(8,128)(2,1)} %bitcast.33) | data formatting | bytes 50331648 | tf_op jit(solution)/shard_map/reshape | solution.py:13
  345.6 78.5 %all-to-all-done = bf16[128,8,4096]{2,1,0:T(8,128)(2,1)} async-done(((bf16[128,8,4096]{2,1,0:T(8,128)(2,1)}), bf16[128,8,4096]{2,1,0:T(8,128)(2,1)}, u32[]{:S(2)}, u32[]{:S(2)}) %all-to-all-start) | async-done | bytes 8388640 | tf_op jit(solution)/shard_map/all_to_all | solution.py:62
  424.1 20.6 %fusion = f32[2,512,1536]{2,1,0:T(8,128)} fusion(bf16[2,4096,1536]{2,1,0:T(8,128)(2,1)} %bitcast.67, bf16[64,2,8,4096]{3,2,1,0:T(8,128)(2,1)} %bitcast.4), kind=kOutput, calls=%fused_computation.1 | convolution fusion | flops 12884901888 | bytes 39845888 | tf_op jit(solution)/shard_map/esd,edc->esc/dot_general | solution.py:21
  444.7 9.2 %multiply_add_fusion = f32[2,768,768]{1,2,0:T(8,128)} fusion(f32[768,768]{0,1:T(8,128)S(1)} %fusion.7, f32[2,512,1536]{2,1,0:T(8,128)} %fusion), kind=kOutput, calls=%fused_computation.7 | convolution fusion | flops 1215037440 | bytes 13369344 | tf_op jit(solution)/shard_map/esf,esg->efg/dot_general | solution.py:29
  454.0 0.2 iota_compare_fusion.1
  454.3 140.2 %all-reduce.3.cloned.1.call-done = f32[2,768,768]{1,2,0:T(8,128)} async-done(((f32[2,768,768]{1,2,0:T(8,128)}), f32[2,768,768]{1,2,0:T(8,128)}) %all-reduce.3.cloned.1.call-update) | async-done | bytes 4718608 | tf_op jit(solution)/shard_map/psum | solution.py:66
  594.4 6.2 copy.75
  600.6 4.4 fusion.3
  605.0 2.1 copy-done.2
  607.1 23.5 %custom-call.49 = f32[2,128,128]{2,1,0:T(8,128)S(1)} custom-call(f32[2,128,128]{2,1,0:T(8,128)S(1)} %cholesky.426), custom_call_target="Cholesky" | custom-call | tf_op jit(solution)/shard_map/jit(cholesky)/cholesky | solution.py:35
  630.6 2.5 cholesky.197
  633.1 19.9 %custom-call.50 = f32[2,1,128,128]{2,3,1,0:T(8,128)S(1)} custom-call(f32[2,1,128,128]{3,2,1,0:T(8,128)S(1)} %select_bitcast_fusion.4), custom_call_target="InvertDiagBlocksLowerTriangular" | custom-call | tf_op jit(solution)/shard_map/jit(cholesky)/cholesky | solution.py:35
  653.0 2.8 constant_dynamic-update-slice_fusion.5
  655.8 1.8 convolution_subtract_fusion
  657.6 23.5 %custom-call.51 = f32[2,128,128]{2,1,0:T(8,128)S(1)} custom-call(f32[2,128,128]{2,1,0:T(8,128)S(1)} %cholesky.430), custom_call_target="Cholesky" | custom-call | tf_op jit(solution)/shard_map/jit(cholesky)/cholesky | solution.py:35
  681.0 0.7 select_bitcast_fusion.3
  681.8 19.7 %custom-call.52 = f32[2,1,128,128]{2,3,1,0:T(8,128)S(1)} custom-call(f32[2,1,128,128]{3,2,1,0:T(8,128)S(1)} %get-tuple-element.18), custom_call_target="InvertDiagBlocksLowerTriangular" | custom-call | tf_op jit(solution)/shard_map/jit(cholesky)/cholesky | solution.py:35
  701.4 1.4 convolution_dynamic-update-slice_fusion
  702.9 2.5 convolution_subtract_fusion.1
  705.4 23.9 %custom-call.53 = f32[2,128,128]{2,1,0:T(8,128)S(1)} custom-call(f32[2,128,128]{2,1,0:T(8,128)S(1)} %cholesky.435), custom_call_target="Cholesky" | custom-call | tf_op jit(solution)/shard_map/jit(cholesky)/cholesky | solution.py:35
  729.3 0.7 select_bitcast_fusion.2
  730.0 19.7 %custom-call.54 = f32[2,1,128,128]{2,3,1,0:T(8,128)S(1)} custom-call(f32[2,1,128,128]{3,2,1,0:T(8,128)S(1)} %get-tuple-element.16), custom_call_target="InvertDiagBlocksLowerTriangular" | custom-call | tf_op jit(solution)/shard_map/jit(cholesky)/cholesky | solution.py:35
  749.6 1.3 convolution_dynamic-update-slice_fusion.1
  751.0 2.7 convolution_subtract_fusion.2
  753.7 23.5 %custom-call.55 = f32[2,128,128]{2,1,0:T(8,128)S(1)} custom-call(f32[2,128,128]{2,1,0:T(8,128)S(1)} %cholesky.440), custom_call_target="Cholesky" | custom-call | tf_op jit(solution)/shard_map/jit(cholesky)/cholesky | solution.py:35
  777.1 0.7 select_bitcast_fusion.1
  777.8 19.8 %custom-call.56 = f32[2,1,128,128]{2,3,1,0:T(8,128)S(1)} custom-call(f32[2,1,128,128]{3,2,1,0:T(8,128)S(1)} %get-tuple-element.14), custom_call_target="InvertDiagBlocksLowerTriangular" | custom-call | tf_op jit(solution)/shard_map/jit(cholesky)/cholesky | solution.py:35
  797.7 1.1 convolution_dynamic-update-slice_fusion.2
  798.8 2.5 convolution_subtract_fusion.3
  801.3 23.5 %custom-call.57 = f32[2,128,128]{2,1,0:T(8,128)S(1)} custom-call(f32[2,128,128]{2,1,0:T(8,128)S(1)} %cholesky.445), custom_call_target="Cholesky" | custom-call | tf_op jit(solution)/shard_map/jit(cholesky)/cholesky | solution.py:35
  824.8 0.7 select_bitcast_fusion
  825.5 19.7 %custom-call.58 = f32[2,1,128,128]{2,3,1,0:T(8,128)S(1)} custom-call(f32[2,1,128,128]{3,2,1,0:T(8,128)S(1)} %get-tuple-element.12), custom_call_target="InvertDiagBlocksLowerTriangular" | custom-call | tf_op jit(solution)/shard_map/jit(cholesky)/cholesky | solution.py:35
  845.1 0.9 convolution_dynamic-update-slice_fusion.3
  846.1 2.2 convolution_subtract_fusion.4
  848.2 23.7 %custom-call.59 = f32[2,128,128]{2,1,0:T(8,128)S(1)} custom-call(f32[2,128,128]{2,1,0:T(8,128)S(1)} %convolution_subtract_fusion.4), custom_call_target="Cholesky" | custom-call | tf_op jit(solution)/shard_map/jit(cholesky)/cholesky | solution.py:35
  871.9 0.7 select_reduce_fusion.4
  873.1 2.1 fusion.6
  875.2 2.0 copy.86
  (34 shorter events, 1.4 us)
Async XLA Ops:
  6.5 34.6 %copy-start = (bf16[64,4096]{1,0:T(8,128)(2,1)S(1)}, bf16[64,4096]{1,0:T(8,128)(2,1)}, u32[]{:S(2)}) copy-start(bf16[64,4096]{1,0:T(8,128)(2,1)} %param.3) | copy-start | bytes 1572868
  27.3 11.9 %copy-start.3 = (s32[64,8]{0,1:T(8,128)S(1)}, s32[64,8]{0,1:T(8,128)}, u32[]{:S(2)}) copy-start(s32[64,8]{0,1:T(8,128)} %param.4) | copy-start | bytes 6148
  27.3 283.6 %all-to-all-start.1 = ((bf16[2,2,4096,768]{3,2,1,0:T(8,128)(2,1)}), bf16[2,2,4096,768]{3,2,1,0:T(8,128)(2,1)}, u32[]{:S(2)}, u32[]{:S(2)}) async-start(bf16[2,2,4096,768]{3,2,1,0:T(8,128)(2,1)} %pad_maximum_fusion), calls=%async_computation.1 | async-start | bytes 50331648 | tf_op jit(solution)/shard_map/all_to_all | solution.py:13
  310.9 113.2 %all-to-all-start = ((bf16[128,8,4096]{2,1,0:T(8,128)(2,1)}), bf16[128,8,4096]{2,1,0:T(8,128)(2,1)}, u32[]{:S(2)}, u32[]{:S(2)}) async-start(bf16[128,8,4096]{2,1,0:T(8,128)(2,1)} %convert_bitcast_fusion), calls=%async_computation | async-start | bytes 16777216 | tf_op jit(solution)/shard_map/all_to_all | solution.py:62
  324.3 270.2 %all-reduce.3.cloned.1.call-start = ((), (), s32[]{:S(2)}) async-start(), calls=%async_computation.2 | async-start | bytes 9437184 | tf_op jit(solution)/shard_map/psum | solution.py:66
  605.0 2.1 copy-start.2
  873.1 4.1 copy-start.1
Sparse Core Ops, SparseCore 0:
  454.1 140.3 all-reduce.2
